TPU v7x, 32 devices: a whole 2x2x4 slice. The times are simulated.
32 devices in a mesh: dp: 16 (over z, x, core), seq: 2 (over y).
Axes of the slice: x: 2, y: 2, z: 4, core: 2. Of those that a mesh axis runs over, the one named last changes fastest.
Arguments:
- tokens: bfloat16 [16, 512, 1152], P('dp', 'seq'), may hold values from -6 to 6
- segment_ids: int32 [16, 512], P('dp'), may hold values from 0 to 3, never falling along the last dimension, each value on 1 to 256 neighbouring positions
- cotangent: bfloat16 [16, 512, 1152], P('dp', 'seq'), may hold values from -6 to 6
- query_weight: bfloat16 [1152, 1024], P(('dp', 'seq')), may hold values from -0.1875 to 0.1875
- key_weight: bfloat16 [1152, 256], P(('dp', 'seq')), may hold values from -0.1875 to 0.1875
- value_weight: bfloat16 [1152, 256], P(('dp', 'seq')), may hold values from -0.1875 to 0.1875
- output_weight: bfloat16 [1024, 1152], P(('dp', 'seq')), may hold values from -0.1875 to 0.1875
- gate_weight: bfloat16 [1152, 6912], P(('dp', 'seq')), may hold values from -0.1875 to 0.1875
- up_weight: bfloat16 [1152, 6912], P(('dp', 'seq')), may hold values from -0.1875 to 0.1875
- down_weight: bfloat16 [6912, 1152], P(('dp', 'seq')), may hold values from -0.078125 to 0.078125
- input_gain: bfloat16 [1152], P(('dp', 'seq')), may hold values from 0.25 to 1.75
- query_gain: bfloat16 [256], P(('dp', 'seq')), may hold values from 0.25 to 1.75
- key_gain: bfloat16 [256], P(('dp', 'seq')), may hold values from 0.25 to 1.75
- attnout_gain: bfloat16 [1152], P(('dp', 'seq')), may hold values from 0.25 to 1.75
- ffnin_gain: bfloat16 [1152], P(('dp', 'seq')), may hold values from 0.25 to 1.75
- ffnout_gain: bfloat16 [1152], P(('dp', 'seq')), may hold values from 0.25 to 1.75
Outputs:
- output: bfloat16 [16, 512, 1152], P('dp', 'seq')
- input_grad: float32 [16, 512, 1152], P('dp', 'seq')
- grad_query: float32 [1152, 1024], P(('dp', 'seq'))
- grad_key: float32 [1152, 256], P(('dp', 'seq'))
- grad_value: float32 [1152, 256], P(('dp', 'seq'))
- grad_output: float32 [1024, 1152], P(('dp', 'seq'))
- grad_gate: float32 [1152, 6912], P(('dp', 'seq'))
- grad_up: float32 [1152, 6912], P(('dp', 'seq'))
- grad_down: float32 [6912, 1152], P(('dp', 'seq'))
- grad_input_gain: float32 [1152], P(('dp', 'seq'))
- grad_query_gain: float32 [256], P(('dp', 'seq'))
- grad_key_gain: float32 [256], P(('dp', 'seq'))
- grad_attnout_gain: float32 [1152], P(('dp', 'seq'))
- grad_ffnin_gain: float32 [1152], P(('dp', 'seq'))
- grad_ffnout_gain: float32 [1152], P(('dp', 'seq'))
Inputs may be any that keep to these rules, and one draw needn't show every extreme that they name: `segment_ids`: in each row the ids never fall and every id occurs; each document spans 1 to 256 positions, one exactly 256.
All inputs are finite; a program needn't handle non-finite values.
Results may differ from a plain program's by a relative error of at most 0.019.
Values may be sent and summed in bfloat16 or wider, within the bound.
A program may use at most 448 MiB of HBM per device.

v0:
```python
import jax
import jax.numpy as jnp
from jax import lax
from jax.sharding import Mesh
from jax.sharding import PartitionSpec as P

epsilon = 1e-06
rope_base = 1000000.0
masked_score = -1e30


def inverse_rms(values):
    return lax.rsqrt(jnp.mean(values * values, axis=-1, keepdims=True) + epsilon)


def rms_back(grad_normed, normed, inverse):
    return inverse * (grad_normed - normed * jnp.mean(grad_normed * normed, axis=-1, keepdims=True))


def doc_positions(segments):
    length = segments.shape[0]
    smaller = segments[None, :] < segments[:, None]
    starts = jnp.sum(smaller.astype(jnp.int32), axis=1)
    return (jnp.arange(length, dtype=jnp.int32) - starts).astype(jnp.float32)


def rope_tables(positions, head_width):
    half_width = head_width // 2
    frequency = rope_base ** (-(2.0 / head_width) * jnp.arange(half_width, dtype=jnp.float32))
    angles = positions[..., None] * frequency
    return (jnp.cos(angles), jnp.sin(angles))


def rotate(values, cos_table, sin_table):
    half_width = values.shape[-1] // 2
    first_half = values[..., :half_width]
    second_half = values[..., half_width:]
    return jnp.concatenate(
        [
            first_half * cos_table - second_half * sin_table,
            second_half * cos_table + first_half * sin_table,
        ],
        axis=-1,
    )


def matmul(left, right):
    return jnp.dot(left, right, preferred_element_type=jnp.float32)


def contract_rows(left, right):
    return lax.dot_general(
        left, right, (((0,), (0,)), ((), ())), preferred_element_type=jnp.float32
    )


def contract_cols(left, right):
    return lax.dot_general(
        left, right, (((1,), (1,)), ((), ())), preferred_element_type=jnp.float32
    )


def gelu_pair(gate_proj, up_proj):
    return jax.nn.gelu(gate_proj, approximate=True) * up_proj


ALL = ("z", "x", "core", "seq")
PLANE = ("x", "core", "seq")


def exchange(blocks, axes):
    return lax.all_to_all(blocks, axes, split_axis=0, concat_axis=0, tiled=True)


def plane_gather(local):
    return lax.all_gather(local, PLANE, axis=0, tiled=True)


def plane_scatter_sum(partial):
    members = lax.axis_size(PLANE)
    terms = exchange(partial.reshape((members, -1) + partial.shape[1:]), PLANE)
    return jnp.sum(terms.astype(jnp.float32), axis=0)


def body(
    tokens,
    segment_ids,
    cotangent,
    query_weight,
    key_weight,
    value_weight,
    output_weight,
    gate_weight,
    up_weight,
    down_weight,
    input_gain,
    query_gain,
    key_gain,
    attnout_gain,
    ffnin_gain,
    ffnout_gain,
):
    bf16, f32 = (jnp.bfloat16, jnp.float32)
    devices = lax.axis_size(ALL)
    members = lax.axis_size(PLANE)
    planes = lax.axis_size("z")
    seq_count = lax.axis_size("seq")
    width_rows = query_weight.shape[0]
    hidden_rows = down_weight.shape[0]
    head_width = key_weight.shape[1]
    query_width = query_weight.shape[1]
    head_count = query_width // head_width
    qkv_width = query_width + 2 * head_width
    mix_rows = output_weight.shape[0]
    padded = (width_rows + 1 + 7) // 8 * 8
    gains = (input_gain, query_gain, key_gain, attnout_gain, ffnin_gain, ffnout_gain)
    gain_row = jnp.concatenate(gains)
    gain_widths = [g.shape[0] for g in gains]
    gain_row = jnp.pad(gain_row, (0, qkv_width - gain_row.shape[0]))
    qkv_local = jnp.concatenate([query_weight, key_weight, value_weight], axis=1)
    packed = jnp.concatenate([qkv_local, gain_row[None]], axis=0)
    packed = jnp.pad(packed, ((0, padded - width_rows - 1), (0, 0)))
    packed_all = lax.all_gather(packed, ALL, axis=0, tiled=False)
    qkv_full = packed_all[:, :width_rows].reshape(devices * width_rows, qkv_width)
    scales, at = ([], 0)
    for width in gain_widths:
        scales.append(packed_all[:, width_rows, at : at + width].reshape(-1).astype(f32))
        at += width
    input_scale, query_scale, key_scale, attnout_scale, ffnin_scale, ffnout_scale = scales
    output_full = lax.all_gather(output_weight, ALL, axis=0, tiled=True)

    def column_blocks(weight):
        pieces = weight.reshape(width_rows, planes, members, hidden_rows)
        return pieces.transpose(2, 0, 1, 3).reshape(members, width_rows, planes * hidden_rows)

    gate_up = jnp.concatenate([column_blocks(gate_weight), column_blocks(up_weight)], axis=1)
    gate_up = jnp.broadcast_to(gate_up[None], (planes,) + gate_up.shape)
    gate_up = exchange(gate_up.reshape((devices,) + gate_up.shape[2:]), ALL)
    gate_full = gate_up[:, :width_rows].reshape(devices * width_rows, planes * hidden_rows)
    up_full = gate_up[:, width_rows:].reshape(devices * width_rows, planes * hidden_rows)
    down_full = exchange(jnp.broadcast_to(down_weight[None], (planes,) + down_weight.shape), "z")
    down_full = down_full.reshape(planes * hidden_rows, down_weight.shape[1])
    hidden = tokens[0].astype(f32)
    incoming = cotangent[0].astype(f32)
    local_rows = hidden.shape[0]
    full_length = local_rows * seq_count
    offset = lax.axis_index("seq") * local_rows
    segment_row = segment_ids[0]

    def mine(rows):
        return lax.dynamic_slice_in_dim(rows, offset, local_rows)

    my_segments = mine(segment_row)
    cos_full, sin_full = rope_tables(doc_positions(segment_row), head_width)
    cos_table, sin_table = (mine(cos_full), mine(sin_full))
    scale = head_width ** (-0.5)
    row_hidden = lax.all_gather(tokens[0], "seq", axis=0, tiled=True).astype(f32)
    row_normed = (row_hidden * inverse_rms(row_hidden) * input_scale).astype(bf16)
    key_value_raw = matmul(row_normed, qkv_full[:, query_width:])
    row_key_raw = key_value_raw[:, :head_width]
    value_rows = key_value_raw[:, head_width:].astype(bf16)
    key_rows = rotate(
        row_key_raw * inverse_rms(row_key_raw) * key_scale, cos_full, sin_full
    ).astype(bf16)
    inv_input = inverse_rms(hidden)
    norm_input = hidden * inv_input
    normed = (norm_input * input_scale).astype(bf16)
    query_raw = matmul(normed, qkv_full[:, :query_width]).reshape(
        local_rows, head_count, head_width
    )
    inv_query = inverse_rms(query_raw)
    norm_query = query_raw * inv_query
    queries = (
        rotate(norm_query * query_scale, cos_table[:, None, :], sin_table[:, None, :]) * scale
    ).astype(bf16)
    key_raw = mine(row_key_raw)
    inv_key = inverse_rms(key_raw)
    norm_key = key_raw * inv_key
    query_places = offset + jnp.arange(local_rows, dtype=jnp.int32)
    key_places = jnp.arange(full_length, dtype=jnp.int32)
    allowed = (my_segments[:, None] == segment_row[None, :]) & (
        query_places[:, None] >= key_places[None, :]
    )
    raw_scores = jnp.einsum("qhd,kd->hqk", queries, key_rows, preferred_element_type=f32)
    scores = jnp.where(allowed[None], raw_scores, masked_score)
    peak = jnp.max(scores, axis=-1, keepdims=True)
    log_total = peak + jnp.log(jnp.sum(jnp.exp(scores - peak), axis=-1, keepdims=True))
    probs = jnp.exp(scores - log_total)
    probs_low = probs.astype(bf16)
    attn_mix = jnp.einsum("hqk,kd->qhd", probs_low, value_rows, preferred_element_type=f32)
    attn_flat = attn_mix.astype(bf16).reshape(local_rows, query_width)
    attn_raw = matmul(attn_flat, output_full)
    inv_attn = inverse_rms(attn_raw)
    norm_attn = attn_raw * inv_attn
    middle = hidden + norm_attn * attnout_scale
    inv_middle = inverse_rms(middle)
    norm_middle = middle * inv_middle
    ffn_in = (norm_middle * ffnin_scale).astype(bf16)
    plane_in = plane_gather(ffn_in)
    gate_proj = matmul(plane_in, gate_full)
    up_proj = matmul(plane_in, up_full)
    activated, gelu_back = jax.vjp(gelu_pair, gate_proj, up_proj)
    activated_low = activated.astype(bf16)
    ffn_raw = plane_scatter_sum(matmul(activated_low, down_full).astype(bf16))
    inv_ffn = inverse_rms(ffn_raw)
    norm_ffn = ffn_raw * inv_ffn
    result = middle + norm_ffn * ffnout_scale
    ffnout_gain_grad = jnp.sum(incoming * norm_ffn, axis=0)
    ffn_raw_grad = rms_back(incoming * ffnout_scale, norm_ffn, inv_ffn).astype(bf16)
    plane_grad = plane_gather(ffn_raw_grad)
    act_grad = contract_cols(plane_grad, down_full)
    gate_grad, up_grad = gelu_back(act_grad)
    gate_low = gate_grad.astype(bf16)
    up_low = up_grad.astype(bf16)
    ffn_in_grad = plane_scatter_sum(
        (contract_cols(gate_low, gate_full) + contract_cols(up_low, up_full)).astype(bf16)
    )
    down_terms = exchange(
        contract_rows(activated_low, plane_grad)
        .astype(bf16)
        .reshape(planes, hidden_rows, down_weight.shape[1]),
        "z",
    )
    down_wgrad = jnp.sum(down_terms.astype(f32), axis=0)

    def row_blocks(grad):
        return grad.astype(bf16).reshape(devices, width_rows, planes * hidden_rows)

    gate_up_terms = exchange(
        jnp.concatenate(
            [
                row_blocks(contract_rows(plane_in, gate_low)),
                row_blocks(contract_rows(plane_in, up_low)),
            ],
            axis=1,
        ),
        ALL,
    )
    gate_up_sum = jnp.sum(
        gate_up_terms.astype(f32).reshape(planes, members, 2, width_rows, planes, hidden_rows),
        axis=0,
    )
    gate_up_sum = gate_up_sum.transpose(1, 2, 3, 0, 4).reshape(
        2, width_rows, planes * members * hidden_rows
    )
    gate_wgrad, up_wgrad = (gate_up_sum[0], gate_up_sum[1])
    ffnin_gain_grad = jnp.sum(ffn_in_grad * norm_middle, axis=0)
    middle_grad = incoming + rms_back(ffn_in_grad * ffnin_scale, norm_middle, inv_middle)
    attnout_gain_grad = jnp.sum(middle_grad * norm_attn, axis=0)
    attn_raw_grad = rms_back(middle_grad * attnout_scale, norm_attn, inv_attn).astype(bf16)
    output_wgrad = contract_rows(attn_flat, attn_raw_grad)
    mix_grad = (
        contract_cols(attn_raw_grad, output_full)
        .astype(bf16)
        .reshape(local_rows, head_count, head_width)
    )
    prob_grad = jnp.einsum("qhd,kd->hqk", mix_grad, value_rows, preferred_element_type=f32)
    row_delta = jnp.sum(prob_grad * probs, axis=-1, keepdims=True)
    score_grad = (probs * (prob_grad - row_delta)).astype(bf16)
    value_grad_rows = jnp.einsum("hqk,qhd->kd", probs_low, mix_grad, preferred_element_type=f32)
    key_grad_rows = jnp.einsum("hqk,qhd->kd", score_grad, queries, preferred_element_type=f32)
    query_grad = jnp.einsum("hqk,kd->qhd", score_grad, key_rows, preferred_element_type=f32)
    key_value_terms = exchange(
        jnp.concatenate([key_grad_rows, value_grad_rows], axis=1)
        .astype(bf16)
        .reshape(seq_count, local_rows, 2 * head_width),
        "seq",
    )
    key_value_grad = jnp.sum(key_value_terms.astype(f32), axis=0)
    key_grad, value_grad = (key_value_grad[:, :head_width], key_value_grad[:, head_width:])
    query_norm_grad = rotate(query_grad * scale, cos_table[:, None, :], -sin_table[:, None, :])
    query_gain_grad = jnp.sum(query_norm_grad * norm_query, axis=(0, 1))
    query_raw_low = (
        rms_back(query_norm_grad * query_scale, norm_query, inv_query)
        .astype(bf16)
        .reshape(local_rows, query_width)
    )
    key_norm_grad = rotate(key_grad, cos_table, -sin_table)
    key_gain_grad = jnp.sum(key_norm_grad * norm_key, axis=0)
    key_raw_low = rms_back(key_norm_grad * key_scale, norm_key, inv_key).astype(bf16)
    qkv_raw_low = jnp.concatenate([query_raw_low, key_raw_low, value_grad.astype(bf16)], axis=1)
    qkv_wgrad = contract_rows(normed, qkv_raw_low)
    normed_grad = contract_cols(qkv_raw_low, qkv_full)
    input_gain_grad = jnp.sum(normed_grad * norm_input, axis=0)
    input_grad = middle_grad + rms_back(normed_grad * input_scale, norm_input, inv_input)

    def to_owners(grad):
        rows, columns = (grad.shape[0] // devices, grad.shape[1])
        blocks = grad.astype(bf16).reshape(planes, members, rows, columns)
        terms = exchange(blocks.transpose(1, 0, 2, 3), PLANE)
        summed = jnp.sum(terms.astype(f32), axis=0).astype(bf16)
        return jnp.sum(exchange(summed, "z").astype(f32), axis=0)

    output_share = to_owners(output_wgrad)
    gain_grads = (
        input_gain_grad,
        query_gain_grad,
        key_gain_grad,
        attnout_gain_grad,
        ffnin_gain_grad,
        ffnout_gain_grad,
    )
    gain_rows = jnp.concatenate([g.reshape(devices, -1) for g in gain_grads], axis=1)
    gain_rows = jnp.pad(gain_rows, ((0, 0), (0, qkv_width - gain_rows.shape[1])))
    qkv_blocks = jnp.concatenate(
        [qkv_wgrad.reshape(devices, width_rows, qkv_width), gain_rows[:, None]], axis=1
    )
    qkv_blocks = jnp.pad(qkv_blocks, ((0, 0), (0, padded - width_rows - 1), (0, 0)))
    qkv_share = to_owners(qkv_blocks.reshape(devices * padded, qkv_width))
    gain_shares, at = ([], 0)
    for width in gain_widths:
        gain_shares.append(qkv_share[width_rows, at : at + width])
        at += width
    return (
        result.astype(bf16)[None],
        input_grad[None],
        qkv_share[:width_rows, :query_width],
        qkv_share[:width_rows, query_width : query_width + head_width],
        qkv_share[:width_rows, query_width + head_width :],
        output_share,
        gate_wgrad,
        up_wgrad,
        down_wgrad,
        *gain_shares,
    )


def solution(mesh):
    dp, seq = (mesh.shape["dp"], mesh.shape["seq"])
    split = Mesh(mesh.devices.reshape(dp // 4, 2, 2, seq), ALL)
    rows = P(("z", "x", "core"), "seq", None)
    matrix, vector = (P(ALL, None), P(ALL))
    return jax.shard_map(
        body,
        mesh=split,
        in_specs=(rows, P(("z", "x", "core"), None), rows) + (matrix,) * 7 + (vector,) * 6,
        out_specs=(rows, rows) + (matrix,) * 7 + (vector,) * 6,
        check_vma=False,
    )
```

profile of v0, /device:TPU:0, one launch (start us, length us, event | category | flops | bytes accessed | tf_op | source)
XLA Modules:
  0.0 778.4 jit_solution(3174932612226022172)
XLA Ops:
  8.0 4.1 concatenate.47
  22.3 7.4 all-to-all-start
  31.6 18.9 %all-gather.14.cloned.1.call-done = bf16[1,512,1152]{2,1,0:T(8,128)(2,1)} async-done(((bf16[1,256,1152]{2,1,0:T(8,128)(2,1)}), bf16[1,512,1152]{2,1,0:T(8,128)(2,1)}) %all-gather.14.cloned.1.call-update) | async-done | bytes 1179664 | tf_op jit(solution)/shard_map/all_gather | solution.py:157
  52.1 88.6 %all-gather.16.cloned.1.call-done = bf16[1280,1536]{1,0:T(8,128)(2,1)} async-done(((bf16[40,1536]{1,0:T(8,128)(2,1)}), bf16[1280,1536]{1,0:T(8,128)(2,1)}) %all-gather.16.cloned.1.call-update) | async-done | bytes 3932176 | tf_op jit(solution)/shard_map/all_gather | solution.py:123
  141.7 5.7 reshape.363
  175.6 24.2 %all-gather.8.cloned.1.call-done = bf16[1024,1152]{1,0:T(8,128)(2,1)} async-done(((bf16[32,1152]{1,0:T(8,128)(2,1)}), bf16[1024,1152]{1,0:T(8,128)(2,1)}) %all-gather.8.cloned.1.call-update) | async-done | bytes 2359312 | tf_op jit(solution)/shard_map/all_gather | solution.py:130
  199.8 3.7 multiply_reduce_fusion.6
  210.0 5.0 all-to-all-start.1
  215.0 5.4 fusion.100
  220.4 4.2 reshape.370
  224.5 4.2 reshape.371
  228.7 16.8 %all-gather.10.cloned.1.call-done = bf16[2048,1152]{1,0:T(8,128)(2,1)} async-done(((bf16[256,1152]{1,0:T(8,128)(2,1)}), bf16[2048,1152]{1,0:T(8,128)(2,1)}) %all-gather.10.cloned.1.call-update) | async-done | bytes 4718608 | tf_op jit(solution)/shard_map/all_gather | solution.py:76
  245.5 7.6 fusion.106
  256.1 9.3 %multiply_convert_fusion.1 = (bf16[2048,864]{0,1:T(8,128)(2,1)}, f32[2048,864]{0,1:T(8,128)}) fusion(f32[2048,864]{0,1:T(8,128)S(1)} %fusion.106, bf16[2048,1152]{1,0:T(8,128)(2,1)S(1)} %copy-done.59, bf16[1152,864]{1,0:T(8,128)(2,1)S(1)} %copy-done.22), kind=kOutput, calls=%fused_computation.17 | convolution fusion | flops 4094558208 | bytes 24403968 | tf_op jit(solution)/shard_map/dot_general | solution.py:48
  265.3 9.2 %convolution_convert_fusion = bf16[2048,1152]{1,0:T(8,128)(2,1)} fusion(bf16[2048,864]{0,1:T(8,128)(2,1)} %get-tuple-element.75, bf16[864,1152]{1,0:T(8,128)(2,1)} %bitcast.18), kind=kOutput, calls=%fused_computation.8 | convolution fusion | flops 4079222784 | bytes 10248192 | tf_op jit(solution)/shard_map/dot_general | solution.py:48
  274.6 4.6 all-to-all-start.2
  280.8 52.2 %all-to-all-done.2 = bf16[8,256,1152]{2,1,0:T(8,128)(2,1)} async-done(((bf16[8,256,1152]{2,1,0:T(8,128)(2,1)}), bf16[8,256,1152]{2,1,0:T(8,128)(2,1)}, u32[]{:S(2)}, u32[]{:S(2)}) %all-to-all-start.2) | async-done | bytes 4718624 | tf_op jit(solution)/shard_map/all_to_all | solution.py:72
  333.1 3.2 convert_reduce_fusion.1
  338.9 39.1 %all-gather.12.cloned.1.call-done = bf16[2048,1152]{1,0:T(8,128)(2,1)} async-done(((bf16[256,1152]{1,0:T(8,128)(2,1)}), bf16[2048,1152]{1,0:T(8,128)(2,1)}) %all-gather.12.cloned.1.call-update) | async-done | bytes 4718608 | tf_op jit(solution)/shard_map/all_gather | solution.py:76
  378.0 14.8 %multiply_convert_fusion = (bf16[2048,864]{0,1:T(8,128)(2,1)S(1)}, bf16[2048,864]{0,1:T(8,128)(2,1)S(1)}) fusion(f32[2048,864]{0,1:T(8,128)} %copy-done.60, f32[2048,864]{0,1:T(8,128)} %get-tuple-element.76, bf16[2048,1152]{1,0:T(8,128)(2,1)} %all-gather.12.cloned.1.call-done, bf16[864,1152]{1,0:T(8,128)(2,1)} %bitcast.18), kind=kOutput, calls=%fused_computation.16 | convolution fusion | flops 4119330816 | bytes 27942912 | tf_op jit(solution)/shard_map/dot_general | solution.py:58
  392.8 5.8 fusion.107
  398.6 7.7 add_convert_fusion
  406.3 4.6 all-to-all-start.3
  413.8 51.0 %all-to-all-done.3 = bf16[8,256,1152]{2,1,0:T(8,128)(2,1)} async-done(((bf16[8,256,1152]{2,1,0:T(8,128)(2,1)}), bf16[8,256,1152]{2,1,0:T(8,128)(2,1)}, u32[]{:S(2)}, u32[]{:S(2)}) %all-to-all-start.3) | async-done | bytes 4718624 | tf_op jit(solution)/shard_map/all_to_all | solution.py:72
  481.7 3.5 all-to-all-start.4
  487.7 5.9 all-to-all-done.4
  494.4 4.0 all-to-all-start.7
  500.9 9.5 %convolution_convert_fusion.5 = bf16[864,1152]{1,0:T(8,128)(2,1)} fusion(bf16[2048,864]{0,1:T(8,128)(2,1)} %get-tuple-element.75, bf16[2048,1152]{1,0:T(8,128)(2,1)} %all-gather.12.cloned.1.call-done), kind=kOutput, calls=%fused_computation.27 | convolution fusion | flops 4077858816 | bytes 10248192 | tf_op jit(solution)/shard_map/dot_general | solution.py:52
  512.0 15.0 %all-to-all-done.7 = bf16[8,4,32,1152]{3,2,1,0:T(8,128)(2,1)S(1)} async-done(((bf16[8,4,32,1152]{3,2,1,0:T(8,128)(2,1)}), bf16[8,4,32,1152]{3,2,1,0:T(8,128)(2,1)S(1)}, u32[]{:S(2)}, u32[]{:S(2)}) %all-to-all-start.7) | async-done | bytes 2359328 | tf_op jit(solution)/shard_map/all_to_all | solution.py:72
  526.9 4.6 all-to-all-start.10
  552.4 3.5 fusion.71
  562.8 4.3 convolution_convert_fusion.1
  568.2 9.6 %all-to-all-done.10 = bf16[4,216,1152]{2,1,0:T(8,128)(2,1)} async-done(((bf16[4,216,1152]{2,1,0:T(8,128)(2,1)}), bf16[4,216,1152]{2,1,0:T(8,128)(2,1)}, u32[]{:S(2)}, u32[]{:S(2)}) %all-to-all-start.10) | async-done | bytes 1990688 | tf_op jit(solution)/shard_map/all_to_all | solution.py:72
  577.8 3.5 all-to-all-start.8
  586.3 4.1 all-to-all-done.8
  590.3 4.7 all-to-all-start.5
  595.0 8.1 %convolution_convert_fusion.3 = bf16[1152,864]{0,1:T(8,128)(2,1)S(1)} fusion(bf16[2048,864]{0,1:T(8,128)(2,1)} %copy-done.62, bf16[2048,1152]{1,0:T(8,128)(2,1)} %all-gather.10.cloned.1.call-done), kind=kOutput, calls=%fused_computation.25 | convolution fusion | flops 4077858816 | bytes 10248192 | tf_op jit(solution)/shard_map/dot_general | solution.py:52
  608.2 9.4 %convolution_convert_fusion.4 = bf16[1152,864]{0,1:T(8,128)(2,1)} fusion(bf16[2048,864]{0,1:T(8,128)(2,1)} %copy-done.61, bf16[2048,1152]{1,0:T(8,128)(2,1)} %all-gather.10.cloned.1.call-done), kind=kOutput, calls=%fused_computation.26 | convolution fusion | flops 4077858816 | bytes 10248192 | tf_op jit(solution)/shard_map/dot_general | solution.py:52
  617.6 4.1 copy.196
  621.6 4.0 reshape.384
  625.6 4.8 pad_maximum_fusion
  630.4 10.1 %all-to-all-done.5 = bf16[8,4,40,1536]{3,2,1,0:T(8,128)(2,1)} async-done(((bf16[8,4,40,1536]{3,2,1,0:T(8,128)(2,1)}), bf16[8,4,40,1536]{3,2,1,0:T(8,128)(2,1)}, u32[]{:S(2)}, u32[]{:S(2)}) %all-to-all-start.5) | async-done | bytes 3932192 | tf_op jit(solution)/shard_map/all_to_all | solution.py:72
  640.5 3.6 all-to-all-start.9
  647.0 3.8 reduce_sum.320
  650.7 86.4 %all-to-all-done.9 = bf16[32,72,864]{2,1,0:T(8,128)(2,1)} async-done(((bf16[32,72,864]{2,1,0:T(8,128)(2,1)}), bf16[32,72,864]{2,1,0:T(8,128)(2,1)}, u32[]{:S(2)}, u32[]{:S(2)}) %all-to-all-start.9) | async-done | bytes 3981344 | tf_op jit(solution)/shard_map/all_to_all | solution.py:72
  737.1 4.3 all-to-all-start.6
  743.5 12.2 %reshape.397 = f32[4,8,2,36,4,216]{5,4,3,2,1,0:T(4,128)} reshape(bf16[32,72,864]{2,1,0:T(8,128)(2,1)} %all-to-all-done.9) | data formatting | bytes 11943936 | tf_op jit(solution)/shard_map/reshape | solution.py:240
  755.7 7.0 reduce_sum.324
  (274 shorter events, 136.4 us)
Async XLA Ops:
  7.2 10.1 %copy-start.28 = (bf16[36,6912]{1,0:T(8,128)(2,1)S(1)}, bf16[36,6912]{1,0:T(8,128)(2,1)}, u32[]{:S(2)}) copy-start(bf16[36,6912]{1,0:T(8,128)(2,1)} %param.23) | copy-start | bytes 1492996
  7.2 43.3 %all-gather.14.cloned.1.call-start = ((), (), s32[]{:S(2)}) async-start(), calls=%async_computation.14 | async-start | bytes 1769472 | tf_op jit(solution)/shard_map/all_gather | solution.py:157
  7.9 132.8 %all-gather.16.cloned.1.call-start = ((), (), s32[]{:S(2)}) async-start(), calls=%async_computation.15 | async-start | bytes 4055040 | tf_op jit(solution)/shard_map/all_gather | solution.py:123
  22.3 8.5 %copy-start.1 = (bf16[1,256,1152]{2,1,0:T(8,128)(2,1)S(1)}, bf16[1,256,1152]{2,1,0:T(8,128)(2,1)}, u32[]{:S(2)}) copy-start(bf16[1,256,1152]{2,1,0:T(8,128)(2,1)} %param.16) | copy-start | bytes 1769476
  22.3 8.8 %copy-start.42 = (s32[1,512]{1,0:T(1,128)S(1)}, s32[1,512]{1,0:T(1,128)}, u32[]{:S(2)}) copy-start(s32[1,512]{1,0:T(1,128)} %param.17) | copy-start | bytes 6148
  22.3 185.2 %all-to-all-start = ((bf16[32,72,864]{2,1,0:T(8,128)(2,1)}), bf16[32,72,864]{2,1,0:T(8,128)(2,1)}, u32[]{:S(2)}, u32[]{:S(2)}) async-start(bf16[32,72,864]{2,1,0:T(8,128)(2,1)} %bitcast.214), calls=%async_computation | async-start | bytes 8257536 | tf_op jit(solution)/shard_map/all_to_all | solution.py:72
  29.7 170.1 %all-gather.8.cloned.1.call-start = ((), (), s32[]{:S(2)}) async-start(), calls=%async_computation.11 | async-start | bytes 2433024 | tf_op jit(solution)/shard_map/all_gather | solution.py:130
  30.5 215.0 %all-gather.10.cloned.1.call-start = ((), (), s32[]{:S(2)}) async-start(), calls=%async_computation.12 | async-start | bytes 5308416 | tf_op jit(solution)/shard_map/all_gather | solution.py:76
  31.1 123.2 %copy-start.54 = (f32[256]{0:T(256)}, f32[256]{0:T(256)S(1)}, u32[]{:S(2)}) copy-start(f32[256]{0:T(256)S(1)} %add_rsqrt_fusion.7) | copy-start | bytes 3076
  31.1 116.3 %copy-start.56 = (s32[1,256]{1,0:T(1,128)}, s32[1,256]{1,0:T(1,128)S(1)}, u32[]{:S(2)}) copy-start(s32[1,256]{1,0:T(1,128)S(1)} %constant_dynamic-slice_fusion.2) | copy-start | bytes 3076
  161.1 13.0 %copy-start.18 = (f32[512,512]{0,1:T(8,128)}, f32[512,512]{0,1:T(8,128)S(1)}, u32[]{:S(2)}) copy-start(f32[512,512]{0,1:T(8,128)S(1)} %fusion.46) | copy-start | bytes 3145732
  174.1 29.4 %copy-start.40 = (f32[4,256]{1,0:T(4,128)}, f32[4,256]{1,0:T(4,128)S(1)}, u32[]{:S(2)}) copy-start(f32[4,256]{1,0:T(4,128)S(1)} %log_add_fusion) | copy-start | bytes 12292
  175.6 28.5 %copy-start.39 = (f32[32,36]{1,0:T(8,128)S(1)}, f32[32,36]{1,0:T(8,128)}, u32[]{:S(2)}) copy-start(f32[32,36]{1,0:T(8,128)} %get-tuple-element.16) | copy-start | bytes 13828
  210.0 55.3 %all-to-all-start.1 = ((bf16[4,216,1152]{2,1,0:T(8,128)(2,1)}), bf16[4,216,1152]{2,1,0:T(8,128)(2,1)}, u32[]{:S(2)}, u32[]{:S(2)}) async-start(bf16[4,216,1152]{2,1,0:T(8,128)(2,1)} %broadcast_in_dim.29), calls=%async_computation.1 | async-start | bytes 3981312 | tf_op jit(solution)/shard_map/all_to_all | solution.py:72
  245.5 10.6 %copy-start.22 = (bf16[1152,864]{1,0:T(8,128)(2,1)S(1)}, bf16[1152,864]{1,0:T(8,128)(2,1)}, u32[]{:S(2)}) copy-start(bf16[1152,864]{1,0:T(8,128)(2,1)} %reshape.371) | copy-start | bytes 5971972
  245.5 10.6 %copy-start.59 = (bf16[2048,1152]{1,0:T(8,128)(2,1)S(1)}, bf16[2048,1152]{1,0:T(8,128)(2,1)}, u32[]{:S(2)}) copy-start(bf16[2048,1152]{1,0:T(8,128)(2,1)} %all-gather.10.cloned.1.call-done) | copy-start | bytes 14155780
  274.6 58.5 %all-to-all-start.2 = ((bf16[8,256,1152]{2,1,0:T(8,128)(2,1)}), bf16[8,256,1152]{2,1,0:T(8,128)(2,1)}, u32[]{:S(2)}, u32[]{:S(2)}) async-start(bf16[8,256,1152]{2,1,0:T(8,128)(2,1)} %bitcast.221), calls=%async_computation.2 | async-start | bytes 9437184 | tf_op jit(solution)/shard_map/all_to_all | solution.py:72
  279.2 98.8 %all-gather.12.cloned.1.call-start = ((), (), s32[]{:S(2)}) async-start(), calls=%async_computation.13 | async-start | bytes 5308416 | tf_op jit(solution)/shard_map/all_gather | solution.py:76
  378.0 14.8 %copy-start.21 = (bf16[1152,864]{1,0:T(8,128)(2,1)S(1)}, bf16[1152,864]{1,0:T(8,128)(2,1)}, u32[]{:S(2)}) copy-start(bf16[1152,864]{1,0:T(8,128)(2,1)} %reshape.370) | copy-start | bytes 5971972
  392.8 5.8 copy-start.61
  392.8 5.8 copy-start.62
  392.8 5.8 copy-start.23
  406.3 58.5 %all-to-all-start.3 = ((bf16[8,256,1152]{2,1,0:T(8,128)(2,1)}), bf16[8,256,1152]{2,1,0:T(8,128)(2,1)}, u32[]{:S(2)}, u32[]{:S(2)}) async-start(bf16[8,256,1152]{2,1,0:T(8,128)(2,1)} %bitcast.220), calls=%async_computation.3 | async-start | bytes 9437184 | tf_op jit(solution)/shard_map/all_to_all | solution.py:72
  478.8 6.5 copy-start.19
  481.7 11.9 %all-to-all-start.4 = ((bf16[2,256,512]{1,2,0:T(8,128)(2,1)}), bf16[2,256,512]{1,2,0:T(8,128)(2,1)S(1)}, u32[]{:S(2)}, u32[]{:S(2)}) async-start(bf16[2,256,512]{1,2,0:T(8,128)(2,1)} %pad_maximum_fusion.4), calls=%async_computation.4 | async-start | bytes 1048576 | tf_op jit(solution)/shard_map/all_to_all | solution.py:72
  493.6 6.5 copy-start.15
  493.6 7.1 copy-start.51
  494.4 32.5 %all-to-all-start.7 = ((bf16[8,4,32,1152]{3,2,1,0:T(8,128)(2,1)}), bf16[8,4,32,1152]{3,2,1,0:T(8,128)(2,1)S(1)}, u32[]{:S(2)}, u32[]{:S(2)}) async-start(bf16[8,4,32,1152]{3,2,1,0:T(8,128)(2,1)} %bitcast.217), calls=%async_computation.7 | async-start | bytes 4718592 | tf_op jit(solution)/shard_map/all_to_all | solution.py:72
  500.9 9.6 %copy-start.14 = (bf16[4,256,512]{1,2,0:T(8,128)(2,1)S(1)}, bf16[4,256,512]{1,2,0:T(8,128)(2,1)}, u32[]{:S(2)}) copy-start(bf16[4,256,512]{1,2,0:T(8,128)(2,1)} %copy-done.13) | copy-start | bytes 3145732
  500.9 9.6 %copy-start.30 = (bf16[512,128]{0,1:T(8,128)(2,1)S(1)}, bf16[512,128]{0,1:T(8,128)(2,1)}, u32[]{:S(2)}) copy-start(bf16[512,128]{0,1:T(8,128)(2,1)} %get-tuple-element.67) | copy-start | bytes 393220
  500.9 9.6 %copy-start.31 = (bf16[512,128]{0,1:T(8,128)(2,1)S(1)}, bf16[512,128]{0,1:T(8,128)(2,1)}, u32[]{:S(2)}) copy-start(bf16[512,128]{0,1:T(8,128)(2,1)} %get-tuple-element.68) | copy-start | bytes 393220
  526.9 50.8 %all-to-all-start.10 = ((bf16[4,216,1152]{2,1,0:T(8,128)(2,1)}), bf16[4,216,1152]{2,1,0:T(8,128)(2,1)}, u32[]{:S(2)}, u32[]{:S(2)}) async-start(bf16[4,216,1152]{2,1,0:T(8,128)(2,1)} %bitcast.232), calls=%async_computation.10 | async-start | bytes 3981312 | tf_op jit(solution)/shard_map/all_to_all | solution.py:72
  531.5 6.6 copy-start.6
  531.5 6.6 copy-start.38
  531.6 6.6 copy-start.49
  541.3 10.7 %copy-start.16 = (f32[512,256]{0,1:T(8,128)S(1)}, f32[512,256]{0,1:T(8,128)}, u32[]{:S(2)}) copy-start(f32[512,256]{0,1:T(8,128)} %get-tuple-element.48) | copy-start | bytes 1572868
  541.3 10.7 %copy-start.47 = (f32[256]{0:T(256)S(1)}, f32[256]{0:T(256)}, u32[]{:S(2)}) copy-start(f32[256]{0:T(256)} %copy-done.46) | copy-start | bytes 3076
  541.3 10.7 %copy-start.57 = (f32[256]{0:T(256)S(1)}, f32[256]{0:T(256)}, u32[]{:S(2)}) copy-start(f32[256]{0:T(256)} %add_rsqrt_fusion.3) | copy-start | bytes 3076
  552.4 4.5 copy-start.2
  552.4 4.5 copy-start.35
  552.4 4.5 copy-start.55
  557.0 5.9 copy-start.33
  577.8 12.5 %all-to-all-start.8 = ((bf16[4,32,1152]{2,1,0:T(8,128)(2,1)}), bf16[4,32,1152]{2,1,0:T(8,128)(2,1)S(1)}, u32[]{:S(2)}, u32[]{:S(2)}) async-start(bf16[4,32,1152]{2,1,0:T(8,128)(2,1)} %reduce_sum.322), calls=%async_computation.8 | async-start | bytes 589824 | tf_op jit(solution)/shard_map/all_to_all | solution.py:72
  590.3 50.2 %all-to-all-start.5 = ((bf16[8,4,40,1536]{3,2,1,0:T(8,128)(2,1)}), bf16[8,4,40,1536]{3,2,1,0:T(8,128)(2,1)}, u32[]{:S(2)}, u32[]{:S(2)}) async-start(bf16[8,4,40,1536]{3,2,1,0:T(8,128)(2,1)} %bitcast.215), calls=%async_computation.5 | async-start | bytes 7864320 | tf_op jit(solution)/shard_map/all_to_all | solution.py:72
  640.5 96.6 %all-to-all-start.9 = ((bf16[32,72,864]{2,1,0:T(8,128)(2,1)}), bf16[32,72,864]{2,1,0:T(8,128)(2,1)}, u32[]{:S(2)}, u32[]{:S(2)}) async-start(bf16[32,72,864]{2,1,0:T(8,128)(2,1)} %pad_maximum_fusion), calls=%async_computation.9 | async-start | bytes 8257536 | tf_op jit(solution)/shard_map/all_to_all | solution.py:72
  647.0 94.5 %copy-start.4 = (f32[256,1152]{1,0:T(8,128)S(1)}, f32[256,1152]{1,0:T(8,128)}, u32[]{:S(2)}) copy-start(f32[256,1152]{1,0:T(8,128)} %copy-done.3) | copy-start | bytes 3538948
  647.0 94.5 %copy-start.10 = (f32[256,1152]{1,0:T(8,128)S(1)}, f32[256,1152]{1,0:T(8,128)}, u32[]{:S(2)}) copy-start(f32[256,1152]{1,0:T(8,128)} %copy-done.9) | copy-start | bytes 3538948
  737.1 31.0 %all-to-all-start.6 = ((bf16[4,40,1536]{2,1,0:T(8,128)(2,1)}), bf16[4,40,1536]{2,1,0:T(8,128)(2,1)}, u32[]{:S(2)}, u32[]{:S(2)}) async-start(bf16[4,40,1536]{2,1,0:T(8,128)(2,1)} %reduce_sum.320), calls=%async_computation.6 | async-start | bytes 983040 | tf_op jit(solution)/shard_map/all_to_all | solution.py:72
  (31 other events, 57.9 us)
Sparse Core Ops, SparseCore 0:
  9.6 40.9 all-gather.13
  54.0 86.6 all-gather.15
  143.6 56.1 all-gather.7
  207.7 37.7 all-gather.9
  339.0 38.8 all-gather.11
where the time goes:
time: 785 us; the launch traced here: 778 us
  waiting for transfers between devices  423 us (54%)
  local copies, waits for them, and re-layouts  114 us (15%)
  matrix products  108 us (14%)
  other arithmetic  67.4 us (9%)
  starting transfers between devices  50.4 us (6%)
  between operations  15.1 us (2%)
    all_to_all x11, waiting for transfers between devices, exchange(): return lax.all_to_all(blocks, axes, split_axis=0, concat_axis=0, tiled=True)  234 us
    all_gather x1, waiting for transfers between devices, body(): packed_all = lax.all_gather(packed, ALL, axis=0, tiled=False)  88.6 us
    all_gather x2, waiting for transfers between devices, plane_gather(): return lax.all_gather(local, PLANE, axis=0, tiled=True)  55.9 us
    all_to_all x11, starting transfers between devices, exchange(): return lax.all_to_all(blocks, axes, split_axis=0, concat_axis=0, tiled=True)  49.7 us
    dot_general x6, matrix products, matmul(): return jnp.dot(left, right, preferred_element_type=jnp.float32)  35.1 us
    dot_general x5, matrix products, contract_cols(): lax.dot_general(left, right, (((1,), (1,)), ((), ())), preferred_element_...  32.7 us
    dot_general x5, matrix products, contract_rows(): lax.dot_general(left, right, (((0,), (0,)), ((), ())), preferred_element_...  32.2 us
    all_gather x1, waiting for transfers between devices, body(): output_full = lax.all_gather(output_weight, ALL, axis=0, tiled=True)  24.2 us
  transfers between devices with their start and end apart: 16, of which 13 were waited for; matrix products, arithmetic and copies ran while one was open for 28% of the time, Pallas kernels for 0%

commit v1 on v0

--- a/solution.py
+++ b/solution.py
@@ -1,3 +1,4 @@
+import functools
 import jax
 import jax.numpy as jnp
 from jax import lax
@@ -7,6 +8,28 @@
 epsilon = 1e-06
 rope_base = 1000000.0
 masked_score = -1e30
+
+
+def _save_stacks_all(s0, link_axis):
+    t_next = jax.lax.axis_size(link_axis)
+    later = jax.lax.axis_index(link_axis)
+    y1, passed, moved = (t_next, later, s0.shape[0])
+    side_arr, x_next = (s0, 1)
+    while x_next < y1:
+        side_arr = jnp.concatenate(
+            [
+                side_arr,
+                jax.lax.ppermute(
+                    side_arr, axis_name=link_axis, perm=[(c, (c - x_next) % y1) for c in range(y1)]
+                ),
+            ],
+            0,
+        )
+        x_next = 2 * x_next
+    return jnp.roll(side_arr, passed * moved, axis=0)
+
+
+point_edges_in = functools.partial(_save_stacks_all, link_axis="seq")
 
 
 def inverse_rms(values):
@@ -154,7 +177,7 @@
     cos_full, sin_full = rope_tables(doc_positions(segment_row), head_width)
     cos_table, sin_table = (mine(cos_full), mine(sin_full))
     scale = head_width ** (-0.5)
-    row_hidden = lax.all_gather(tokens[0], "seq", axis=0, tiled=True).astype(f32)
+    row_hidden = point_edges_in(tokens[0]).astype(f32)
     row_normed = (row_hidden * inverse_rms(row_hidden) * input_scale).astype(bf16)
     key_value_raw = matmul(row_normed, qkv_full[:, query_width:])
     row_key_raw = key_value_raw[:, :head_width]

time: 785 us -> 755 us (0.962)
  waiting for transfers between devices: 423 us -> 382 us
    all_gather x1, waiting for transfers between devices: 88.6 us -> 69.4 us  [body(): packed_all = lax.all_gather(packed, ALL, axis=0, tiled=False)]
    all_gather x1 -> x0, waiting for transfers between devices: 18.9 us -> none  [body(): lax.all_gather(tokens[0], 'seq', axis=0, tiled=True).astype(f32)]
  transfers between devices with their start and end apart: 16 -> 16, of which waited for: 13 -> 12; matrix products, arithmetic and copies ran while one was open for 28% -> 30% of each run, Pallas kernels for 0% -> 0%
where the time goes in v1:
time: 755 us; the launch traced here: 748 us
  waiting for transfers between devices  382 us (51%)
  local copies, waits for them, and re-layouts  120 us (16%)
  matrix products  108 us (14%)
  other arithmetic  71.1 us (9%)
  starting transfers between devices  51 us (7%)
  between operations  15.1 us (2%)
    all_to_all x11, waiting for transfers between devices, exchange(): return lax.all_to_all(blocks, axes, split_axis=0, concat_axis=0, tiled=True)  233 us
    all_gather x1, waiting for transfers between devices, body(): packed_all = lax.all_gather(packed, ALL, axis=0, tiled=False)  69.4 us
    all_gather x2, waiting for transfers between devices, plane_gather(): return lax.all_gather(local, PLANE, axis=0, tiled=True)  56.1 us
    all_to_all x11, starting transfers between devices, exchange(): return lax.all_to_all(blocks, axes, split_axis=0, concat_axis=0, tiled=True)  47.1 us
    dot_general x5, matrix products, contract_cols(): lax.dot_general(left, right, (((1,), (1,)), ((), ())), preferred_element_...  34.7 us
    dot_general x6, matrix products, matmul(): return jnp.dot(left, right, preferred_element_type=jnp.float32)  34.7 us
    dot_general x5, matrix products, contract_rows(): lax.dot_general(left, right, (((0,), (0,)), ((), ())), preferred_element_...  32 us
    all_gather x1, waiting for transfers between devices, body(): output_full = lax.all_gather(output_weight, ALL, axis=0, tiled=True)  22.3 us
  transfers between devices with their start and end apart: 16, of which 12 were waited for; matrix products, arithmetic and copies ran while one was open for 30% of the time, Pallas kernels for 0%

profile of v1, /device:TPU:0, one launch (start us, length us, event | category | flops | bytes accessed | tf_op | source)
XLA Modules:
  0.0 747.7 jit_solution(5580783710138876210)
XLA Ops:
  7.2 4.1 concatenate.54
  24.7 5.0 all-to-all-start
  36.2 69.4 %all-gather.12.cloned.1.call-done = bf16[1280,1536]{1,0:T(8,128)(2,1)} async-done(((bf16[40,1536]{1,0:T(8,128)(2,1)}), bf16[1280,1536]{1,0:T(8,128)(2,1)}) %all-gather.12.cloned.1.call-update) | async-done | bytes 3932176 | tf_op jit(solution)/shard_map/all_gather | solution.py:146
  107.2 3.9 reshape.363
  115.9 4.3 copy.164
  146.2 22.3 %all-gather.6.cloned.1.call-done = bf16[1024,1152]{1,0:T(8,128)(2,1)} async-done(((bf16[32,1152]{1,0:T(8,128)(2,1)}), bf16[1024,1152]{1,0:T(8,128)(2,1)}) %all-gather.6.cloned.1.call-update) | async-done | bytes 2359312 | tf_op jit(solution)/shard_map/all_gather | solution.py:153
  168.5 3.5 multiply_reduce_fusion.6
  177.5 4.6 all-to-all-start.1
  182.1 5.5 fusion.97
  187.5 4.2 reshape.370
  191.7 4.2 reshape.371
  195.9 17.1 %all-gather.8.cloned.1.call-done = bf16[2048,1152]{1,0:T(8,128)(2,1)} async-done(((bf16[256,1152]{1,0:T(8,128)(2,1)}), bf16[2048,1152]{1,0:T(8,128)(2,1)}) %all-gather.8.cloned.1.call-update) | async-done | bytes 4718608 | tf_op jit(solution)/shard_map/all_gather | solution.py:99
  212.9 7.6 %fusion.103 = f32[2048,864]{0,1:T(8,128)S(1)} fusion(bf16[2048,1152]{1,0:T(8,128)(2,1)} %all-gather.8.cloned.1.call-done, bf16[1152,864]{1,0:T(8,128)(2,1)} %reshape.370), kind=kOutput, calls=%fused_computation.224 | convolution fusion | flops 4076863488 | bytes 13787136 | tf_op jit(solution)/shard_map/dot_general | solution.py:71
  223.5 9.2 %multiply_convert_fusion.1 = (bf16[2048,864]{0,1:T(8,128)(2,1)}, f32[2048,864]{0,1:T(8,128)}) fusion(f32[2048,864]{0,1:T(8,128)S(1)} %fusion.103, bf16[2048,1152]{1,0:T(8,128)(2,1)S(1)} %copy-done.60, bf16[1152,864]{1,0:T(8,128)(2,1)S(1)} %copy-done.26), kind=kOutput, calls=%fused_computation.17 | convolution fusion | flops 4094558208 | bytes 24403968 | tf_op jit(solution)/shard_map/dot_general | solution.py:71
  232.7 9.2 %convolution_convert_fusion = bf16[2048,1152]{1,0:T(8,128)(2,1)} fusion(bf16[2048,864]{0,1:T(8,128)(2,1)} %get-tuple-element.78, bf16[864,1152]{1,0:T(8,128)(2,1)} %bitcast.16), kind=kOutput, calls=%fused_computation.8 | convolution fusion | flops 4079222784 | bytes 10248192 | tf_op jit(solution)/shard_map/dot_general | solution.py:71
  241.9 4.7 all-to-all-start.2
  247.1 53.5 %all-to-all-done.2 = bf16[8,256,1152]{2,1,0:T(8,128)(2,1)} async-done(((bf16[8,256,1152]{2,1,0:T(8,128)(2,1)}), bf16[8,256,1152]{2,1,0:T(8,128)(2,1)}, u32[]{:S(2)}, u32[]{:S(2)}) %all-to-all-start.2) | async-done | bytes 4718624 | tf_op jit(solution)/shard_map/all_to_all | solution.py:95
  300.6 3.2 convert_reduce_fusion.1
  306.4 39.1 %all-gather.10.cloned.1.call-done = bf16[2048,1152]{1,0:T(8,128)(2,1)} async-done(((bf16[256,1152]{1,0:T(8,128)(2,1)}), bf16[2048,1152]{1,0:T(8,128)(2,1)}) %all-gather.10.cloned.1.call-update) | async-done | bytes 4718608 | tf_op jit(solution)/shard_map/all_gather | solution.py:99
  345.5 14.8 %multiply_convert_fusion = (bf16[2048,864]{0,1:T(8,128)(2,1)S(1)}, bf16[2048,864]{0,1:T(8,128)(2,1)S(1)}) fusion(f32[2048,864]{0,1:T(8,128)} %copy-done.61, f32[2048,864]{0,1:T(8,128)} %get-tuple-element.79, bf16[2048,1152]{1,0:T(8,128)(2,1)} %all-gather.10.cloned.1.call-done, bf16[864,1152]{1,0:T(8,128)(2,1)} %bitcast.16), kind=kOutput, calls=%fused_computation.16 | convolution fusion | flops 4119330816 | bytes 27942912 | tf_op jit(solution)/shard_map/dot_general | solution.py:81
  360.3 5.8 fusion.104
  366.1 7.9 %add_convert_fusion = bf16[2048,1152]{1,0:T(8,128)(2,1)} fusion(f32[2048,1152]{1,0:T(8,128)S(1)} %fusion.104, bf16[2048,864]{0,1:T(8,128)(2,1)S(1)} %get-tuple-element.38, bf16[1152,864]{1,0:T(8,128)(2,1)S(1)} %copy-done.27), kind=kOutput, calls=%fused_computation.3 | convolution fusion | flops 4081582080 | bytes 19685376 | tf_op jit(solution)/shard_map/dot_general | solution.py:81
  374.0 4.7 all-to-all-start.3
  381.9 50.8 %all-to-all-done.3 = bf16[8,256,1152]{2,1,0:T(8,128)(2,1)} async-done(((bf16[8,256,1152]{2,1,0:T(8,128)(2,1)}), bf16[8,256,1152]{2,1,0:T(8,128)(2,1)}, u32[]{:S(2)}, u32[]{:S(2)}) %all-to-all-start.3) | async-done | bytes 4718624 | tf_op jit(solution)/shard_map/all_to_all | solution.py:95
  449.5 3.5 all-to-all-start.4
  455.5 5.9 all-to-all-done.4
  462.2 3.8 all-to-all-start.7
  468.0 9.5 %convolution_convert_fusion.5 = bf16[864,1152]{1,0:T(8,128)(2,1)} fusion(bf16[2048,864]{0,1:T(8,128)(2,1)} %get-tuple-element.78, bf16[2048,1152]{1,0:T(8,128)(2,1)} %all-gather.10.cloned.1.call-done), kind=kOutput, calls=%fused_computation.27 | convolution fusion | flops 4077858816 | bytes 10248192 | tf_op jit(solution)/shard_map/dot_general | solution.py:75
  485.7 8.8 %all-to-all-done.7 = bf16[8,4,32,1152]{3,2,1,0:T(8,128)(2,1)S(1)} async-done(((bf16[8,4,32,1152]{3,2,1,0:T(8,128)(2,1)}), bf16[8,4,32,1152]{3,2,1,0:T(8,128)(2,1)S(1)}, u32[]{:S(2)}, u32[]{:S(2)}) %all-to-all-start.7) | async-done | bytes 2359328 | tf_op jit(solution)/shard_map/all_to_all | solution.py:95
  494.5 4.6 all-to-all-start.10
  513.7 5.4 fusion.38
  529.3 4.0 convolution_convert_fusion.1
  534.5 10.9 %all-to-all-done.10 = bf16[4,216,1152]{2,1,0:T(8,128)(2,1)} async-done(((bf16[4,216,1152]{2,1,0:T(8,128)(2,1)}), bf16[4,216,1152]{2,1,0:T(8,128)(2,1)}, u32[]{:S(2)}, u32[]{:S(2)}) %all-to-all-start.10) | async-done | bytes 1990688 | tf_op jit(solution)/shard_map/all_to_all | solution.py:95
  545.4 3.5 all-to-all-start.8
  553.9 4.1 all-to-all-done.8
  557.9 4.7 all-to-all-start.5
  562.7 8.1 %convolution_convert_fusion.3 = bf16[1152,864]{0,1:T(8,128)(2,1)S(1)} fusion(bf16[2048,864]{0,1:T(8,128)(2,1)} %copy-done.63, bf16[2048,1152]{1,0:T(8,128)(2,1)} %all-gather.8.cloned.1.call-done), kind=kOutput, calls=%fused_computation.25 | convolution fusion | flops 4077858816 | bytes 10248192 | tf_op jit(solution)/shard_map/dot_general | solution.py:75
  575.8 9.4 %convolution_convert_fusion.4 = bf16[1152,864]{0,1:T(8,128)(2,1)} fusion(bf16[2048,864]{0,1:T(8,128)(2,1)} %copy-done.62, bf16[2048,1152]{1,0:T(8,128)(2,1)} %all-gather.8.cloned.1.call-done), kind=kOutput, calls=%fused_computation.26 | convolution fusion | flops 4077858816 | bytes 10248192 | tf_op jit(solution)/shard_map/dot_general | solution.py:75
  585.2 4.1 copy.196
  589.3 4.0 reshape.384
  593.3 4.8 pad_maximum_fusion
  598.1 10.1 %all-to-all-done.5 = bf16[8,4,40,1536]{3,2,1,0:T(8,128)(2,1)} async-done(((bf16[8,4,40,1536]{3,2,1,0:T(8,128)(2,1)}), bf16[8,4,40,1536]{3,2,1,0:T(8,128)(2,1)}, u32[]{:S(2)}, u32[]{:S(2)}) %all-to-all-start.5) | async-done | bytes 3932192 | tf_op jit(solution)/shard_map/all_to_all | solution.py:95
  608.1 3.6 all-to-all-start.9
  611.7 3.6 reduce_sum.320
  615.3 89.4 %all-to-all-done.9 = bf16[32,72,864]{2,1,0:T(8,128)(2,1)} async-done(((bf16[32,72,864]{2,1,0:T(8,128)(2,1)}), bf16[32,72,864]{2,1,0:T(8,128)(2,1)}, u32[]{:S(2)}, u32[]{:S(2)}) %all-to-all-start.9) | async-done | bytes 3981344 | tf_op jit(solution)/shard_map/all_to_all | solution.py:95
  704.7 4.4 all-to-all-start.6
  712.7 12.2 %reshape.397 = f32[4,8,2,36,4,216]{5,4,3,2,1,0:T(4,128)} reshape(bf16[32,72,864]{2,1,0:T(8,128)(2,1)} %all-to-all-done.9) | data formatting | bytes 11943936 | tf_op jit(solution)/shard_map/reshape | solution.py:263
  724.9 7.0 reduce_sum.324
  (274 shorter events, 144.7 us)
Async XLA Ops:
  7.2 12.5 %copy-start.33 = (bf16[36,6912]{1,0:T(8,128)(2,1)S(1)}, bf16[36,6912]{1,0:T(8,128)(2,1)}, u32[]{:S(2)}) copy-start(bf16[36,6912]{1,0:T(8,128)(2,1)} %param.23) | copy-start | bytes 1492996
  7.2 98.4 %all-gather.12.cloned.1.call-start = ((), (), s32[]{:S(2)}) async-start(), calls=%async_computation.14 | async-start | bytes 4055040 | tf_op jit(solution)/shard_map/all_gather | solution.py:146
  13.0 20.4 %collective-permute-start = (bf16[256,1152]{1,0:T(8,128)(2,1)}, bf16[256,1152]{1,0:T(8,128)(2,1)S(1)}, u32[]{:S(2)}, u32[]{:S(2)}) collective-permute-start(bf16[256,1152]{1,0:T(8,128)(2,1)} %bitcast.185), channel_id=1, source_target_pairs={{0,1},{1,0},{2,3},{3,2},{4,5},{5,4},{6,7},{7,6},{8,9},{9,8},{10,11... | collective-permute-start | bytes 1769480 | tf_op jit(solution)/shard_map/ppermute | solution.py:22
  24.7 6.3 copy-start.6
  24.7 6.6 copy-start.45
  24.7 150.3 %all-to-all-start = ((bf16[32,72,864]{2,1,0:T(8,128)(2,1)}), bf16[32,72,864]{2,1,0:T(8,128)(2,1)}, u32[]{:S(2)}, u32[]{:S(2)}) async-start(bf16[32,72,864]{2,1,0:T(8,128)(2,1)} %bitcast.180), calls=%async_computation | async-start | bytes 8257536 | tf_op jit(solution)/shard_map/all_to_all | solution.py:95
  29.7 138.8 %all-gather.6.cloned.1.call-start = ((), (), s32[]{:S(2)}) async-start(), calls=%async_computation.11 | async-start | bytes 2433024 | tf_op jit(solution)/shard_map/all_gather | solution.py:153
  30.4 182.5 %all-gather.8.cloned.1.call-start = ((), (), s32[]{:S(2)}) async-start(), calls=%async_computation.12 | async-start | bytes 5308416 | tf_op jit(solution)/shard_map/all_gather | solution.py:99
  31.2 76.0 %copy-start.55 = (s32[256]{0:T(256)}, s32[256]{0:T(256)S(1)}, u32[]{:S(2)}) copy-start(s32[256]{0:T(256)S(1)} %iota_add_fusion) | copy-start | bytes 3076
  31.3 93.1 %copy-start.57 = (f32[256]{0:T(256)}, f32[256]{0:T(256)S(1)}, u32[]{:S(2)}) copy-start(f32[256]{0:T(256)S(1)} %add_rsqrt_fusion.7) | copy-start | bytes 3076
  31.3 75.9 %copy-start.52 = (s32[1,256]{1,0:T(1,128)}, s32[1,256]{1,0:T(1,128)S(1)}, u32[]{:S(2)}) copy-start(s32[1,256]{1,0:T(1,128)S(1)} %constant_dynamic-slice_fusion.2) | copy-start | bytes 3076
  111.1 23.9 %copy-start.3 = (bf16[1152,1536]{1,0:T(8,128)(2,1)}, bf16[1152,1536]{1,0:T(8,128)(2,1)S(1)}, u32[]{:S(2)}) copy-start(bf16[1152,1536]{1,0:T(8,128)(2,1)S(1)} %reshape.363) | copy-start | bytes 10616836
  146.2 26.0 %copy-start.18 = (bf16[256,4,256]{2,0,1:T(8,128)(2,1)}, bf16[256,4,256]{2,0,1:T(8,128)(2,1)S(1)}, u32[]{:S(2)}) copy-start(bf16[256,4,256]{2,0,1:T(8,128)(2,1)S(1)} %convolution_convert_fusion.7) | copy-start | bytes 1572868
  146.2 25.9 %copy-start.44 = (f32[32,36]{1,0:T(8,128)S(1)}, f32[32,36]{1,0:T(8,128)}, u32[]{:S(2)}) copy-start(f32[32,36]{1,0:T(8,128)} %get-tuple-element.16) | copy-start | bytes 13828
  177.5 55.2 %all-to-all-start.1 = ((bf16[4,216,1152]{2,1,0:T(8,128)(2,1)}), bf16[4,216,1152]{2,1,0:T(8,128)(2,1)}, u32[]{:S(2)}, u32[]{:S(2)}) async-start(bf16[4,216,1152]{2,1,0:T(8,128)(2,1)} %broadcast_in_dim.29), calls=%async_computation.1 | async-start | bytes 3981312 | tf_op jit(solution)/shard_map/all_to_all | solution.py:95
  212.9 10.6 %copy-start.26 = (bf16[1152,864]{1,0:T(8,128)(2,1)S(1)}, bf16[1152,864]{1,0:T(8,128)(2,1)}, u32[]{:S(2)}) copy-start(bf16[1152,864]{1,0:T(8,128)(2,1)} %reshape.371) | copy-start | bytes 5971972
  212.9 10.6 %copy-start.60 = (bf16[2048,1152]{1,0:T(8,128)(2,1)S(1)}, bf16[2048,1152]{1,0:T(8,128)(2,1)}, u32[]{:S(2)}) copy-start(bf16[2048,1152]{1,0:T(8,128)(2,1)} %all-gather.8.cloned.1.call-done) | copy-start | bytes 14155780
  241.9 5.0 copy-start.43
  241.9 58.6 %all-to-all-start.2 = ((bf16[8,256,1152]{2,1,0:T(8,128)(2,1)}), bf16[8,256,1152]{2,1,0:T(8,128)(2,1)}, u32[]{:S(2)}, u32[]{:S(2)}) async-start(bf16[8,256,1152]{2,1,0:T(8,128)(2,1)} %bitcast.189), calls=%async_computation.2 | async-start | bytes 9437184 | tf_op jit(solution)/shard_map/all_to_all | solution.py:95
  246.7 98.8 %all-gather.10.cloned.1.call-start = ((), (), s32[]{:S(2)}) async-start(), calls=%async_computation.13 | async-start | bytes 5308416 | tf_op jit(solution)/shard_map/all_gather | solution.py:99
  345.5 14.8 %copy-start.25 = (bf16[1152,864]{1,0:T(8,128)(2,1)S(1)}, bf16[1152,864]{1,0:T(8,128)(2,1)}, u32[]{:S(2)}) copy-start(bf16[1152,864]{1,0:T(8,128)(2,1)} %reshape.370) | copy-start | bytes 5971972
  360.3 5.8 copy-start.62
  360.3 5.8 copy-start.63
  360.3 5.8 copy-start.27
  374.0 4.8 copy-start.53
  374.0 4.8 copy-start.56
  374.0 58.6 %all-to-all-start.3 = ((bf16[8,256,1152]{2,1,0:T(8,128)(2,1)}), bf16[8,256,1152]{2,1,0:T(8,128)(2,1)}, u32[]{:S(2)}, u32[]{:S(2)}) async-start(bf16[8,256,1152]{2,1,0:T(8,128)(2,1)} %bitcast.188), calls=%async_computation.3 | async-start | bytes 9437184 | tf_op jit(solution)/shard_map/all_to_all | solution.py:95
  446.6 6.5 copy-start.19
  449.5 11.9 %all-to-all-start.4 = ((bf16[2,256,512]{1,2,0:T(8,128)(2,1)}), bf16[2,256,512]{1,2,0:T(8,128)(2,1)S(1)}, u32[]{:S(2)}, u32[]{:S(2)}) async-start(bf16[2,256,512]{1,2,0:T(8,128)(2,1)} %pad_maximum_fusion.4), calls=%async_computation.4 | async-start | bytes 1048576 | tf_op jit(solution)/shard_map/all_to_all | solution.py:95
  461.4 5.1 copy-start.42
  461.4 5.9 copy-start.51
  462.2 32.3 %all-to-all-start.7 = ((bf16[8,4,32,1152]{3,2,1,0:T(8,128)(2,1)}), bf16[8,4,32,1152]{3,2,1,0:T(8,128)(2,1)S(1)}, u32[]{:S(2)}, u32[]{:S(2)}) async-start(bf16[8,4,32,1152]{3,2,1,0:T(8,128)(2,1)} %bitcast.183), calls=%async_computation.7 | async-start | bytes 4718592 | tf_op jit(solution)/shard_map/all_to_all | solution.py:95
  468.0 9.5 %copy-start.13 = (bf16[4,256,512]{1,2,0:T(8,128)(2,1)S(1)}, bf16[4,256,512]{1,2,0:T(8,128)(2,1)}, u32[]{:S(2)}) copy-start(bf16[4,256,512]{1,2,0:T(8,128)(2,1)} %copy-done.12) | copy-start | bytes 3145732
  468.0 9.6 %copy-start.37 = (bf16[512,128]{0,1:T(8,128)(2,1)S(1)}, bf16[512,128]{0,1:T(8,128)(2,1)}, u32[]{:S(2)}) copy-start(bf16[512,128]{0,1:T(8,128)(2,1)} %copy-done.36) | copy-start | bytes 393220
  468.0 9.6 %copy-start.39 = (bf16[512,128]{0,1:T(8,128)(2,1)S(1)}, bf16[512,128]{0,1:T(8,128)(2,1)}, u32[]{:S(2)}) copy-start(bf16[512,128]{0,1:T(8,128)(2,1)} %copy-done.38) | copy-start | bytes 393220
  478.6 5.2 copy-start.5
  478.6 5.2 copy-start.50
  494.5 50.9 %all-to-all-start.10 = ((bf16[4,216,1152]{2,1,0:T(8,128)(2,1)}), bf16[4,216,1152]{2,1,0:T(8,128)(2,1)}, u32[]{:S(2)}, u32[]{:S(2)}) async-start(bf16[4,216,1152]{2,1,0:T(8,128)(2,1)} %bitcast.200), calls=%async_computation.10 | async-start | bytes 3981312 | tf_op jit(solution)/shard_map/all_to_all | solution.py:95
  499.1 11.3 %copy-start.22 = (f32[256,128]{0,1:T(8,128)S(1)}, f32[256,128]{0,1:T(8,128)}, u32[]{:S(2)}) copy-start(f32[256,128]{0,1:T(8,128)} %copy-done.21) | copy-start | bytes 393220
  501.4 10.0 %copy-start.14 = (f32[512,256]{0,1:T(8,128)S(1)}, f32[512,256]{0,1:T(8,128)}, u32[]{:S(2)}) copy-start(f32[512,256]{0,1:T(8,128)} %get-tuple-element.50) | copy-start | bytes 1572868
  501.4 10.0 %copy-start.48 = (f32[256]{0:T(256)S(1)}, f32[256]{0:T(256)}, u32[]{:S(2)}) copy-start(f32[256]{0:T(256)} %reshape.390) | copy-start | bytes 3076
  503.5 10.2 %copy-start.46 = (f32[1152]{0:T(1024)S(1)}, f32[1152]{0:T(1024)}, u32[]{:S(2)}) copy-start(f32[1152]{0:T(1024)} %reshape.389) | copy-start | bytes 13828
  513.7 9.2 %copy-start.2 = (f32[256,1152]{1,0:T(8,128)S(1)}, f32[256,1152]{1,0:T(8,128)}, u32[]{:S(2)}) copy-start(f32[256,1152]{1,0:T(8,128)} %copy-done.1) | copy-start | bytes 3538948
  533.4 15.5 %copy-start.32 = (bf16[32,1,1536]{2,1,0:T(2,128)(2,1)S(1)}, bf16[32,1,1536]{2,1,0:T(2,128)(2,1)}, u32[]{:S(2)}) copy-start(bf16[32,1,1536]{2,1,0:T(2,128)(2,1)} %copy.193) | copy-start | bytes 294916
  545.4 12.5 %all-to-all-start.8 = ((bf16[4,32,1152]{2,1,0:T(8,128)(2,1)}), bf16[4,32,1152]{2,1,0:T(8,128)(2,1)S(1)}, u32[]{:S(2)}, u32[]{:S(2)}) async-start(bf16[4,32,1152]{2,1,0:T(8,128)(2,1)} %reduce_sum.322), calls=%async_computation.8 | async-start | bytes 589824 | tf_op jit(solution)/shard_map/all_to_all | solution.py:95
  557.9 50.2 %all-to-all-start.5 = ((bf16[8,4,40,1536]{3,2,1,0:T(8,128)(2,1)}), bf16[8,4,40,1536]{3,2,1,0:T(8,128)(2,1)}, u32[]{:S(2)}, u32[]{:S(2)}) async-start(bf16[8,4,40,1536]{3,2,1,0:T(8,128)(2,1)} %bitcast.181), calls=%async_computation.5 | async-start | bytes 7864320 | tf_op jit(solution)/shard_map/all_to_all | solution.py:95
  608.1 96.6 %all-to-all-start.9 = ((bf16[32,72,864]{2,1,0:T(8,128)(2,1)}), bf16[32,72,864]{2,1,0:T(8,128)(2,1)}, u32[]{:S(2)}, u32[]{:S(2)}) async-start(bf16[32,72,864]{2,1,0:T(8,128)(2,1)} %pad_maximum_fusion), calls=%async_computation.9 | async-start | bytes 8257536 | tf_op jit(solution)/shard_map/all_to_all | solution.py:95
  704.7 32.5 %all-to-all-start.6 = ((bf16[4,40,1536]{2,1,0:T(8,128)(2,1)}), bf16[4,40,1536]{2,1,0:T(8,128)(2,1)}, u32[]{:S(2)}, u32[]{:S(2)}) async-start(bf16[4,40,1536]{2,1,0:T(8,128)(2,1)} %reduce_sum.320), calls=%async_computation.6 | async-start | bytes 983040 | tf_op jit(solution)/shard_map/all_to_all | solution.py:95
  (32 other events, 62.0 us)
Sparse Core Ops, SparseCore 0:
  13.1 92.3 all-gather.11
  108.5 59.9 all-gather.5
  175.1 37.7 all-gather.7
  306.5 38.8 all-gather.9
